TPU v7x, 256 devices: a whole 4x4x8 slice. The times are simulated.
256 devices in a mesh: pix: 32 (over z_hi, y, x), tm: 8 (over z_lo, core).
Axes of the slice: x: 4, y: 4, z: 8 (z_hi: 2, z_lo: 4; z = z_hi * 4 + z_lo), core: 2. Of those that a mesh axis runs over, the one named last changes fastest.
Arguments:
- fields: float32 [256, 8, 2, 1024], P('pix', None, None, 'tm'), may hold values from -6 to 6
- profiles: bfloat16 [65536, 256], P('pix'), may hold values from -0.75 to 0.75
- phase: float32 [256, 1024], P(('pix', 'tm')), may hold values from -3.140625 to 3.140625
Outputs:
- advanced: float32 [256, 8, 2, 1024], P('pix', None, None, 'tm')
All inputs are finite; a program needn't handle non-finite values.
Results may differ from a plain program's by a relative error of at most 0.003.
Values may be sent and summed in bfloat16 or wider, within the bound.
A program may use at most 64 MiB of HBM per device.

v0:
```python
import math
import jax
import jax.numpy as jnp
from jax import lax
from jax.sharding import PartitionSpec as P


def joined_along(blocks, dim):
    blocks = jnp.moveaxis(blocks, 0, dim)
    dims = blocks.shape
    return blocks.reshape(*dims[:dim], dims[dim] * dims[dim + 1], *dims[dim + 2 :])


def copy_for_each(value, axis):
    devices = lax.axis_size(axis)
    return lax.all_to_all(
        jnp.broadcast_to(value[None], (devices, *value.shape)), axis, 0, 0, tiled=True
    )


def gathered_copies(value, axis, dim):
    return joined_along(copy_for_each(value, axis), dim)


def in_blocks(value, dim, devices):
    dims = value.shape
    blocks = value.reshape(*dims[:dim], devices, dims[dim] // devices, *dims[dim + 1 :])
    return jnp.moveaxis(blocks, dim, 0)


def summed_on_arrival(value, axis, dim):
    blocks = in_blocks(value, dim, lax.axis_size(axis))
    arrived = lax.all_to_all(blocks, axis, split_axis=0, concat_axis=0, tiled=True)
    return arrived.astype(jnp.float32).sum(axis=0)


def split_length(length):
    first = 2 ** ((length.bit_length() - 1) // 2)
    return (first, length // first)


def small_table(size):
    index = jnp.arange(size, dtype=jnp.int32)
    product = index[:, None] * index[None, :] % size
    angles = product.astype(jnp.float32) * (2.0 * math.pi / size)
    return (jnp.cos(angles), jnp.sin(angles))


def twiddles(first, second, length):
    rows = jnp.arange(first, dtype=jnp.int32)
    cols = jnp.arange(second, dtype=jnp.int32)
    product = rows[:, None] * cols[None, :] % length
    angles = product.astype(jnp.float32) * (2.0 * math.pi / length)
    return (jnp.cos(angles), jnp.sin(angles))


def contract_last(values, table):
    return jnp.einsum(
        "mbkv,vq->mbkq",
        values,
        table,
        precision=lax.Precision.HIGHEST,
        preferred_element_type=jnp.float32,
    )


def contract_third(values, table):
    return jnp.einsum(
        "mbuv,uk->mbkv",
        values,
        table,
        precision=lax.Precision.HIGHEST,
        preferred_element_type=jnp.float32,
    )


def dispersed(values, phase_rows, length):
    first, second = split_length(length)
    cos_first, sin_first = small_table(first)
    cos_second, sin_second = small_table(second)
    twist_cos, twist_sin = twiddles(first, second, length)
    modes_here = values.shape[0]
    batch = values.shape[1]
    real_part = values[:, :, 0].reshape(modes_here, batch, first, second)
    imag_part = values[:, :, 1].reshape(modes_here, batch, first, second)
    section_re = contract_third(real_part, cos_first) + contract_third(imag_part, sin_first)
    section_im = contract_third(imag_part, cos_first) - contract_third(real_part, sin_first)
    turned_re = section_re * twist_cos + section_im * twist_sin
    turned_im = section_im * twist_cos - section_re * twist_sin
    freq_re = contract_last(turned_re, cos_second) + contract_last(turned_im, sin_second)
    freq_im = contract_last(turned_im, cos_second) - contract_last(turned_re, sin_second)
    ordered = jnp.transpose(phase_rows.reshape(modes_here, second, first), (0, 2, 1))[:, None]
    phase_cos = jnp.cos(ordered)
    phase_sin = jnp.sin(ordered)
    spun_re = freq_re * phase_cos - freq_im * phase_sin
    spun_im = freq_re * phase_sin + freq_im * phase_cos
    back_re = contract_last(spun_re, cos_second) - contract_last(spun_im, sin_second)
    back_im = contract_last(spun_im, cos_second) + contract_last(spun_re, sin_second)
    again_re = back_re * twist_cos - back_im * twist_sin
    again_im = back_im * twist_cos + back_re * twist_sin
    out_re = contract_third(again_re, cos_first) - contract_third(again_im, sin_first)
    out_im = contract_third(again_im, cos_first) + contract_third(again_re, sin_first)
    out_re = out_re.reshape(modes_here, batch, length) / length
    out_im = out_im.reshape(modes_here, batch, length) / length
    return jnp.stack([out_re, out_im], axis=2)


def body(fields, profiles, phase):
    mode_local = fields.shape[0]
    batch = fields.shape[1]
    time_local = fields.shape[3]
    pixel_local = profiles.shape[0]
    length = time_local * lax.axis_size("tm")
    scale = 1.0 / math.sqrt(pixel_local * lax.axis_size("pix"))
    modal = fields.astype(jnp.bfloat16)
    piece = gathered_copies(modal, "pix", 0)
    columns = profiles
    spatial = jnp.dot(
        columns, piece.reshape(piece.shape[0], -1), preferred_element_type=jnp.float32
    )
    spatial = spatial.reshape(pixel_local, batch, 2, time_local)
    real_part = spatial[:, :, 0]
    imag_part = spatial[:, :, 1]
    power = real_part * real_part + imag_part * imag_part
    nonlin = (
        jnp.stack([power * real_part, power * imag_part], axis=2)
        .astype(jnp.bfloat16)
        .reshape(pixel_local, -1)
    )
    columns = profiles
    kerr = summed_on_arrival(
        lax.dot_general(
            columns, nonlin, (((0,), (0,)), ((), ())), preferred_element_type=jnp.float32
        ).astype(jnp.bfloat16),
        "pix",
        0,
    )
    kerr = kerr.reshape(mode_local, batch, 2, time_local) * scale
    stepped = jnp.stack([fields[:, :, 0] - kerr[:, :, 1], fields[:, :, 1] + kerr[:, :, 0]], axis=2)
    result = dispersed(
        lax.all_to_all(stepped, "tm", split_axis=0, concat_axis=3, tiled=True), phase, length
    )
    return lax.all_to_all(result, "tm", split_axis=3, concat_axis=0, tiled=True)


def solution(mesh):
    return jax.shard_map(
        body,
        mesh=mesh,
        in_specs=(P("pix", None, None, "tm"), P("pix", None), P(("pix", "tm"), None)),
        out_specs=P("pix", None, None, "tm"),
        check_vma=False,
    )
```

profile of v0, /device:TPU:1, one launch (start us, length us, event | category | flops | bytes accessed | tf_op | source)
XLA Modules:
  0.0 126.4 jit_solution(6760236970866442374)
XLA Ops:
  0.0 1.0 convert_element_type.76
  1.0 0.9 broadcast_in_dim.2
  1.9 35.3 %all_to_all.46 = bf16[32,8,8,2,128]{4,3,2,1,0:T(2,128)(2,1)S(1)} all-to-all(bf16[32,8,8,2,128]{4,3,2,1,0:T(2,128)(2,1)S(1)} %broadcast_in_dim.2), channel_id=1, replica_groups=mesh['pix'=32,'tm'=8] {'pix'}, dimensions={0} | all-to-all | bytes 2097152 | tf_op jit(solution)/shard_map/all_to_all | solution.py:16
  37.2 0.8 reshape_reshape.3
  38.0 0.5 copy.59
  38.6 2.4 %fusion.7 = f32[2048,8,2,128]{0,3,2,1:T(8,128)S(1)} fusion(bf16[8,2,128,256]{3,2,1,0:T(8,128)(2,1)S(1)} %bitcast.110, bf16[2048,256]{1,0:T(8,128)(2,1)S(1)} %copy-done), kind=kOutput, calls=%fused_computation.21 | convolution fusion | flops 2147483648 | bytes 18874368 | tf_op jit(solution)/shard_map/dot_general | solution.py:118
  40.9 3.7 %multiply_convert_fusion.1 = (bf16[2048,8,1,128]{0,3,2,1:T(8,128)(2,1)S(1)}, bf16[2048,8,1,128]{0,3,2,1:T(8,128)(2,1)}) fusion(f32[2048,8,2,128]{0,3,2,1:T(8,128)S(1)} %fusion.7), kind=kLoop, calls=%fused_computation.2 | loop fusion | flops 14680064 | bytes 25165824 | tf_op jit(solution)/shard_map/convert
  44.7 6.2 %pad_maximum_fusion = bf16[2048,8,2,128]{0,3,2,1:T(8,128)(2,1)} fusion(bf16[2048,8,1,128]{0,3,2,1:T(8,128)(2,1)} %get-tuple-element.10, bf16[2048,8,1,128]{0,3,2,1:T(8,128)(2,1)S(1)} %get-tuple-element.9), kind=kLoop, calls=%fused_computation | loop fusion | flops 4194304 | bytes 16777216 | tf_op jit(solution)/shard_map/stack | solution.py:126
  50.8 6.9 %fusion = bf16[32,8,2048]{2,1,0:T(8,128)(2,1)} fusion(bf16[2048,2048]{0,1:T(8,128)(2,1)} %bitcast.109, bf16[2048,256]{1,0:T(8,128)(2,1)S(1)} %copy-done), kind=kOutput, calls=%fused_computation.5 | convolution fusion | flops 2148007936 | bytes 10485760 | tf_op jit(solution)/shard_map/dot_general | solution.py:132
  57.7 4.5 %all-to-all-start.1 = ((bf16[32,8,2048]{2,1,0:T(8,128)(2,1)}), bf16[32,8,2048]{2,1,0:T(8,128)(2,1)S(1)}, u32[]{:S(2)}, u32[]{:S(2)}) async-start(bf16[32,8,2048]{2,1,0:T(8,128)(2,1)} %fusion), calls=%async_computation.1 | async-start | bytes 2097152 | tf_op jit(solution)/shard_map/all_to_all | solution.py:33
  62.2 0.1 fusion.49
  62.3 15.6 %all-to-all-done.1 = bf16[32,8,2048]{2,1,0:T(8,128)(2,1)S(1)} async-done(((bf16[32,8,2048]{2,1,0:T(8,128)(2,1)}), bf16[32,8,2048]{2,1,0:T(8,128)(2,1)S(1)}, u32[]{:S(2)}, u32[]{:S(2)}) %all-to-all-start.1) | async-done | bytes 1048608 | tf_op jit(solution)/shard_map/all_to_all | solution.py:33
  77.9 0.2 convert_reduce_fusion
  78.2 0.7 pad_maximum_fusion.1
  78.9 21.8 %all-to-all-start.2 = ((f32[8,8,2,128]{3,2,1,0:T(2,128)}), f32[8,8,2,128]{3,2,1,0:T(2,128)S(1)}, u32[]{:S(2)}, u32[]{:S(2)}) async-start(f32[8,8,2,128]{3,2,1,0:T(2,128)} %pad_maximum_fusion.1), calls=%async_computation.2 | async-start | bytes 131072 | tf_op jit(solution)/shard_map/all_to_all | solution.py:141
  100.7 0.1 fusion.48
  101.0 0.2 cosine_reduce_fusion
  101.2 0.1 copy.65
  101.4 4.4 %all-to-all-done.2 = f32[8,8,2,128]{3,2,1,0:T(2,128)S(1)} async-done(((f32[8,8,2,128]{3,2,1,0:T(2,128)}), f32[8,8,2,128]{3,2,1,0:T(2,128)S(1)}, u32[]{:S(2)}, u32[]{:S(2)}) %all-to-all-start.2) | async-done | bytes 65568 | tf_op jit(solution)/shard_map/all_to_all | solution.py:141
  105.8 0.2 slice_reduce_fusion
  106.0 0.1 reshape.185
  106.1 0.3 fusion.37
  106.4 0.1 reshape.184
  106.5 0.3 fusion.39
  106.9 0.3 fusion.1
  107.2 0.3 fusion.2
  107.6 0.3 fusion.10
  107.9 0.3 fusion.12
  108.3 0.3 convolution_add_fusion.2
  108.6 0.3 convolution_subtract_fusion.2
  109.0 0.3 fusion.16
  109.3 0.3 fusion.15
  109.6 0.3 convolution_add_fusion.1
  110.0 0.3 convolution_subtract_fusion.1
  110.3 0.4 fusion.17
  110.7 0.3 fusion.18
  111.0 0.3 fusion.4
  111.4 0.1 div.21
  111.5 0.4 fusion.6
  111.9 0.1 div.25
  112.0 0.5 copy.75
  112.5 1.6 %reshape.213 = f32[8,1,2048]{2,1,0:T(1,128)S(1)} reshape(f32[1024,1,2,8]{3,2,1,0:T(2,128)S(1)} %bitcast.112) | data formatting | bytes 131072
  114.1 8.3 %all_to_all.47 = f32[8,1,2048]{2,1,0:T(1,128)S(1)} all-to-all(f32[8,1,2048]{2,1,0:T(1,128)S(1)} %reshape.213), channel_id=1, replica_groups=mesh['pix'=32,'tm'=8] {'tm'}, dimensions={0} | all-to-all | bytes 131072 | tf_op jit(solution)/shard_map/all_to_all | solution.py:143
  122.4 0.5 broadcast.240
  122.9 0.8 reduce.12
  123.7 1.6 %reshape.214 = f32[1024,1,2,8]{3,2,1,0:T(2,128)S(1)} reshape(f32[8,2048]{1,0:T(8,128)S(1)} %reduce.12) | data formatting | bytes 131072
  125.3 0.4 copy.76
  125.8 0.7 copy.77
  (16 shorter events, 0.5 us)
Async XLA Ops:
  0.0 38.5 %copy-start = (bf16[2048,256]{1,0:T(8,128)(2,1)S(1)}, bf16[2048,256]{1,0:T(8,128)(2,1)}, u32[]{:S(2)}) copy-start(bf16[2048,256]{1,0:T(8,128)(2,1)} %param.4) | copy-start | bytes 3145732
  50.8 27.3 %copy-start.1 = (f32[8,8,2,128]{3,2,1,0:T(2,128)S(1)}, f32[8,8,2,128]{3,2,1,0:T(2,128)}, u32[]{:S(2)}) copy-start(f32[8,8,2,128]{3,2,1,0:T(2,128)} %param.3) | copy-start | bytes 196612
  50.8 50.1 %copy-start.2 = (f32[1,1024]{1,0:T(1,128)S(1)}, f32[1,1024]{1,0:T(1,128)}, u32[]{:S(2)}) copy-start(f32[1,1024]{1,0:T(1,128)} %param.5) | copy-start | bytes 12292
  57.7 20.2 %all-to-all-start.1 = ((bf16[32,8,2048]{2,1,0:T(8,128)(2,1)}), bf16[32,8,2048]{2,1,0:T(8,128)(2,1)S(1)}, u32[]{:S(2)}, u32[]{:S(2)}) async-start(bf16[32,8,2048]{2,1,0:T(8,128)(2,1)} %fusion), calls=%async_computation.1 | async-start | bytes 2097152 | tf_op jit(solution)/shard_map/all_to_all | solution.py:33
  78.9 26.9 %all-to-all-start.2 = ((f32[8,8,2,128]{3,2,1,0:T(2,128)}), f32[8,8,2,128]{3,2,1,0:T(2,128)S(1)}, u32[]{:S(2)}, u32[]{:S(2)}) async-start(f32[8,8,2,128]{3,2,1,0:T(2,128)} %pad_maximum_fusion.1), calls=%async_computation.2 | async-start | bytes 131072 | tf_op jit(solution)/shard_map/all_to_all | solution.py:141
where the time goes:
time: 127 us; the launch traced here: 126 us
  blocking collectives  43.6 us (34%)
  starting transfers between devices  26.3 us (21%)
  waiting for transfers between devices  20 us (16%)
  matrix products  14.7 us (12%)
  other arithmetic  12.7 us (10%)
  local copies, waits for them, and re-layouts  8.85 us (7%)
    all_to_all x1, blocking collectives, copy_for_each(): lax.all_to_all(jnp.broadcast_to(value[None], (devices, *value.shape)), ax...  35.3 us
    all_to_all x1, starting transfers between devices, body(): lax.all_to_all(stepped, 'tm', split_axis=0, concat_axis=3, tiled=True)  21.8 us
    all_to_all x1, waiting for transfers between devices, summed_on_arrival(): lax.all_to_all(blocks, axis, split_axis=0, concat_axis=0, tiled=True)  15.6 us
    all_to_all x1, blocking collectives, body(): return lax.all_to_all(result, 'tm', split_axis=3, concat_axis=0, tiled=True)  8.29 us
    dot_general x1, matrix products, body(): lax.dot_general(columns, nonlin, (((0,), (0,)), ((), ())), preferred_elem...  6.85 us
    another operation x1, other arithmetic, body(): jnp.stack([power * real_part, power * imag_part], axis=2)  6.18 us
    all_to_all x1, starting transfers between devices, summed_on_arrival(): lax.all_to_all(blocks, axis, split_axis=0, concat_axis=0, tiled=True)  4.52 us
    all_to_all x1, waiting for transfers between devices, body(): lax.all_to_all(stepped, 'tm', split_axis=0, concat_axis=3, tiled=True)  4.38 us
  transfers between devices with their start and end apart: 2, of which 2 were waited for; matrix products, arithmetic and copies ran while one was open for 1% of the time, Pallas kernels for 0%

commit v1 on v0

--- a/solution.py
+++ b/solution.py
@@ -138,7 +138,12 @@
     kerr = kerr.reshape(mode_local, batch, 2, time_local) * scale
     stepped = jnp.stack([fields[:, :, 0] - kerr[:, :, 1], fields[:, :, 1] + kerr[:, :, 0]], axis=2)
     result = dispersed(
-        lax.all_to_all(stepped, "tm", split_axis=0, concat_axis=3, tiled=True), phase, length
+        jnp.concatenate(
+            lax.all_to_all(jnp.stack(jnp.split(stepped, lax.axis_size("tm"), axis=0)), "tm", 0, 0),
+            axis=3,
+        ),
+        phase,
+        length,
     )
     return lax.all_to_all(result, "tm", split_axis=3, concat_axis=0, tiled=True)
 

time: 127 us -> 131 us (1.031)
  local copies, waits for them, and re-layouts: 8.85 us -> 13.6 us
    unnamed x8 -> x15, local copies, waits for them, and re-layouts: 3.19 us -> 7.39 us
where the time goes in v1:
time: 131 us
  blocking collectives  43.6 us (33%)
  starting transfers between devices  26.3 us (20%)
  waiting for transfers between devices  20 us (15%)
  matrix products  14.7 us (11%)
  local copies, waits for them, and re-layouts  13.6 us (10%)
  other arithmetic  12.1 us (9%)
    all_to_all x1, blocking collectives, copy_for_each(): lax.all_to_all(jnp.broadcast_to(value[None], (devices, *value.shape)), ax...  35.3 us
    all_to_all x1, starting transfers between devices, body(): lax.all_to_all(jnp.stack(jnp.split(stepped, lax.axis_size('tm'), axis=0))...  21.8 us
    all_to_all x1, waiting for transfers between devices, summed_on_arrival(): lax.all_to_all(blocks, axis, split_axis=0, concat_axis=0, tiled=True)  15.6 us
    all_to_all x1, blocking collectives, body(): return lax.all_to_all(result, 'tm', split_axis=3, concat_axis=0, tiled=True)  8.29 us
    unnamed x15, local copies, waits for them, and re-layouts  7.39 us
    dot_general x1, matrix products, body(): lax.dot_general(columns, nonlin, (((0,), (0,)), ((), ())), preferred_elem...  6.85 us
    another operation x1, other arithmetic, body(): jnp.stack([power * real_part, power * imag_part], axis=2)  6.18 us
    all_to_all x1, starting transfers between devices, summed_on_arrival(): lax.all_to_all(blocks, axis, split_axis=0, concat_axis=0, tiled=True)  4.52 us
  transfers between devices with their start and end apart: 2, of which 2 were waited for; matrix products, arithmetic and copies ran while one was open for 1% of the time, Pallas kernels for 0%

profile of v1, /device:TPU:1, one launch (start us, length us, event | category | flops | bytes accessed | tf_op | source)
XLA Modules:
  0.0 130.6 jit_solution(15973376103596795433)
XLA Ops:
  0.0 1.0 convert_element_type.76
  1.0 0.9 broadcast_in_dim.2
  1.9 35.3 %all_to_all.33 = bf16[32,8,8,2,128]{4,3,2,1,0:T(2,128)(2,1)S(1)} all-to-all(bf16[32,8,8,2,128]{4,3,2,1,0:T(2,128)(2,1)S(1)} %broadcast_in_dim.2), channel_id=1, replica_groups=mesh['pix'=32,'tm'=8] {'pix'}, dimensions={0} | all-to-all | bytes 2097152 | tf_op jit(solution)/shard_map/all_to_all | solution.py:16
  37.2 0.8 reshape_reshape.3
  38.0 0.5 copy.71
  38.6 2.4 %fusion.7 = f32[2048,8,2,128]{0,3,2,1:T(8,128)S(1)} fusion(bf16[8,2,128,256]{3,2,1,0:T(8,128)(2,1)S(1)} %bitcast.130, bf16[2048,256]{1,0:T(8,128)(2,1)S(1)} %copy-done), kind=kOutput, calls=%fused_computation.21 | convolution fusion | flops 2147483648 | bytes 18874368 | tf_op jit(solution)/shard_map/dot_general | solution.py:118
  40.9 3.7 %multiply_convert_fusion.1 = (bf16[2048,8,1,128]{0,3,2,1:T(8,128)(2,1)S(1)}, bf16[2048,8,1,128]{0,3,2,1:T(8,128)(2,1)}) fusion(f32[2048,8,2,128]{0,3,2,1:T(8,128)S(1)} %fusion.7), kind=kLoop, calls=%fused_computation.2 | loop fusion | flops 14680064 | bytes 25165824 | tf_op jit(solution)/shard_map/convert
  44.7 6.2 %pad_maximum_fusion = bf16[2048,8,2,128]{0,3,2,1:T(8,128)(2,1)} fusion(bf16[2048,8,1,128]{0,3,2,1:T(8,128)(2,1)} %get-tuple-element.10, bf16[2048,8,1,128]{0,3,2,1:T(8,128)(2,1)S(1)} %get-tuple-element.9), kind=kLoop, calls=%fused_computation | loop fusion | flops 4194304 | bytes 16777216 | tf_op jit(solution)/shard_map/stack | solution.py:126
  50.8 6.9 %fusion = bf16[32,8,2048]{2,1,0:T(8,128)(2,1)} fusion(bf16[2048,2048]{0,1:T(8,128)(2,1)} %bitcast.129, bf16[2048,256]{1,0:T(8,128)(2,1)S(1)} %copy-done), kind=kOutput, calls=%fused_computation.5 | convolution fusion | flops 2148007936 | bytes 10485760 | tf_op jit(solution)/shard_map/dot_general | solution.py:132
  57.7 4.5 %all-to-all-start.1 = ((bf16[32,8,2048]{2,1,0:T(8,128)(2,1)}), bf16[32,8,2048]{2,1,0:T(8,128)(2,1)S(1)}, u32[]{:S(2)}, u32[]{:S(2)}) async-start(bf16[32,8,2048]{2,1,0:T(8,128)(2,1)} %fusion), calls=%async_computation.1 | async-start | bytes 2097152 | tf_op jit(solution)/shard_map/all_to_all | solution.py:33
  62.3 15.6 %all-to-all-done.1 = bf16[32,8,2048]{2,1,0:T(8,128)(2,1)S(1)} async-done(((bf16[32,8,2048]{2,1,0:T(8,128)(2,1)}), bf16[32,8,2048]{2,1,0:T(8,128)(2,1)S(1)}, u32[]{:S(2)}, u32[]{:S(2)}) %all-to-all-start.1) | async-done | bytes 1048608 | tf_op jit(solution)/shard_map/all_to_all | solution.py:33
  77.9 0.2 convert_reduce_fusion
  78.3 0.6 constant_dynamic-update-slice_fusion.7
  78.9 0.6 constant_dynamic-update-slice_fusion.6
  79.5 0.6 constant_dynamic-update-slice_fusion.5
  80.1 0.6 constant_dynamic-update-slice_fusion.4
  80.7 0.6 constant_dynamic-update-slice_fusion.3
  81.3 0.6 constant_dynamic-update-slice_fusion.2
  81.9 0.6 constant_dynamic-update-slice_fusion.1
  82.5 0.6 constant_dynamic-update-slice_fusion
  83.1 21.8 %all-to-all-start.2 = ((f32[8,1,8,2,128]{4,1,3,2,0:T(1,128)}), f32[8,1,8,2,128]{4,1,3,2,0:T(1,128)S(1)}, u32[]{:S(2)}, u32[]{:S(2)}) async-start(f32[8,1,8,2,128]{4,1,3,2,0:T(1,128)} %constant_dynamic-update-slice_fusion), calls=%async_computation.2 | async-start | bytes 131072 | tf_op jit(solution)/shard_map/all_to_all | solution.py:142
  105.1 0.2 cosine_reduce_fusion
  105.6 4.4 %all-to-all-done.2 = f32[8,1,8,2,128]{4,1,3,2,0:T(1,128)S(1)} async-done(((f32[8,1,8,2,128]{4,1,3,2,0:T(1,128)}), f32[8,1,8,2,128]{4,1,3,2,0:T(1,128)S(1)}, u32[]{:S(2)}, u32[]{:S(2)}) %all-to-all-start.2) | async-done | bytes 65568 | tf_op jit(solution)/shard_map/all_to_all | solution.py:142
  110.0 0.2 slice_reduce_fusion
  110.3 0.3 fusion.37
  110.7 0.3 fusion.39
  111.1 0.3 fusion.1
  111.4 0.3 fusion.2
  111.8 0.3 fusion.10
  112.1 0.3 fusion.12
  112.4 0.3 convolution_add_fusion.2
  112.8 0.3 convolution_subtract_fusion.2
  113.1 0.3 fusion.16
  113.5 0.3 fusion.15
  113.8 0.3 convolution_add_fusion.1
  114.2 0.3 convolution_subtract_fusion.1
  114.5 0.4 fusion.17
  114.9 0.3 fusion.18
  115.2 0.3 fusion.4
  115.7 0.4 fusion.6
  116.2 0.5 copy.94
  116.7 1.6 %reshape.221 = f32[8,1,2048]{2,1,0:T(1,128)S(1)} reshape(f32[1024,1,2,8]{3,2,1,0:T(2,128)S(1)} %bitcast.132) | data formatting | bytes 131072
  118.3 8.3 %all_to_all.34 = f32[8,1,2048]{2,1,0:T(1,128)S(1)} all-to-all(f32[8,1,2048]{2,1,0:T(1,128)S(1)} %reshape.221), channel_id=1, replica_groups=mesh['pix'=32,'tm'=8] {'tm'}, dimensions={0} | all-to-all | bytes 131072 | tf_op jit(solution)/shard_map/all_to_all | solution.py:148
  126.6 0.5 broadcast.240
  127.1 0.8 reduce.12
  127.9 1.6 %reshape.222 = f32[1024,1,2,8]{3,2,1,0:T(2,128)S(1)} reshape(f32[8,2048]{1,0:T(8,128)S(1)} %reduce.12) | data formatting | bytes 131072
  129.5 0.4 copy.95
  129.9 0.7 copy.96
  (24 shorter events, 1.2 us)
Async XLA Ops:
  0.0 38.5 %copy-start = (bf16[2048,256]{1,0:T(8,128)(2,1)S(1)}, bf16[2048,256]{1,0:T(8,128)(2,1)}, u32[]{:S(2)}) copy-start(bf16[2048,256]{1,0:T(8,128)(2,1)} %param.4) | copy-start | bytes 3145732
  50.8 27.3 %copy-start.1 = (f32[8,8,2,128]{3,2,1,0:T(2,128)S(1)}, f32[8,8,2,128]{3,2,1,0:T(2,128)}, u32[]{:S(2)}) copy-start(f32[8,8,2,128]{3,2,1,0:T(2,128)} %param.3) | copy-start | bytes 196612
  50.8 54.3 %copy-start.2 = (f32[1,1024]{1,0:T(1,128)S(1)}, f32[1,1024]{1,0:T(1,128)}, u32[]{:S(2)}) copy-start(f32[1,1024]{1,0:T(1,128)} %param.5) | copy-start | bytes 12292
  57.7 20.2 %all-to-all-start.1 = ((bf16[32,8,2048]{2,1,0:T(8,128)(2,1)}), bf16[32,8,2048]{2,1,0:T(8,128)(2,1)S(1)}, u32[]{:S(2)}, u32[]{:S(2)}) async-start(bf16[32,8,2048]{2,1,0:T(8,128)(2,1)} %fusion), calls=%async_computation.1 | async-start | bytes 2097152 | tf_op jit(solution)/shard_map/all_to_all | solution.py:33
  83.1 26.9 %all-to-all-start.2 = ((f32[8,1,8,2,128]{4,1,3,2,0:T(1,128)}), f32[8,1,8,2,128]{4,1,3,2,0:T(1,128)S(1)}, u32[]{:S(2)}, u32[]{:S(2)}) async-start(f32[8,1,8,2,128]{4,1,3,2,0:T(1,128)} %constant_dynamic-update-slice_fusion), calls=%async_computation.2 | async-start | bytes 131072 | tf_op jit(solution)/shard_map/all_to_all | solution.py:142
